TPU v7x, 256 devices: a whole 4x4x8 slice. The times are simulated.
256 devices in a mesh: vox: 64 (over y, x, z_lo), sen: 4 (over z_hi, core).
Axes of the slice: x: 4, y: 4, z: 8 (z_hi: 2, z_lo: 4; z = z_hi * 4 + z_lo), core: 2. Of those that a mesh axis runs over, the one named last changes fastest.
Arguments:
- image: float32 [64, 2, 512], P('vox'), may hold values from -6 to 6
- weights: bfloat16 [64, 4, 5, 1024, 1024], P('vox', 'sen'), may hold values from -0.0625 to 0.0625
- block_ids: int32 [64, 4, 5], P('vox', 'sen'), may hold values from 0 to 15
- offsets: int32 [64, 4, 5], P('vox', 'sen'), may hold values from 0 to 1984
- counts: int32 [64, 4], P('vox', 'sen'), may hold values from 1 to 5, as said below
- measured: bfloat16 [4, 256, 2048], P('sen', 'vox'), may hold values from -6 to 6
Outputs:
- image_next: float32 [64, 2, 512], P('vox')
- residual: float32 [4, 256, 2048], P('sen', 'vox')
Inputs may be any that keep to these rules, and one draw needn't show every extreme that they name: `counts`: some slab and group has all 5 slots live in every draw.
All inputs are finite; a program needn't handle non-finite values.
Results may differ from a plain program's by a relative error of at most 0.0025.
Values may be sent and summed in bfloat16 or wider, within the bound.
No kernel may reach another device: no remote copies, remote signals or barrier semaphores. Data moves between devices by JAX's collectives and lax.ppermute only.
A program may use at most 64 MiB of HBM per device.

v0:
```python
import jax
import jax.numpy as jnp
from jax import lax
from jax.sharding import PartitionSpec as P

SENSORS = 1024
SAMPLES = 2048
SB = 16
WIN = 64
K_MAX = 5
TAPS = ((-2, 1.0 / 12.0), (-1, -8.0 / 12.0), (1, 8.0 / 12.0), (2, -1.0 / 12.0))
STEP_SIZE = 0.25
TV_WEIGHT = 0.3
TV_EPS = 0.01


def extended(array, sides, width):
    for axis, dim in sides:
        count, length = (lax.axis_size(axis), array.shape[dim])
        up = [(i, (i + 1) % count) for i in range(count - 1)]
        down = [(j, i) for i, j in up]
        last = lax.slice_in_dim(array, length - width, length, axis=dim)
        initial = lax.slice_in_dim(array, 0, width, axis=dim)
        before = lax.ppermute(last, axis, up)
        after = lax.ppermute(initial, axis, down)
        array = jnp.concatenate([before, array, after], axis=dim)
    return array


def derivative(signal):
    length_t = signal.shape[-1]
    padded = jnp.pad(signal, [(0, 0)] * (signal.ndim - 1) + [(2, 2)])
    summed = jnp.zeros_like(signal)
    for shift_by, coefficient in TAPS:
        summed = summed + coefficient * padded[..., 2 + shift_by : 2 + shift_by + length_t]
    return summed


def forward_step(volume, axis_dim):
    length_a = volume.shape[axis_dim]
    ahead = jnp.concatenate(
        [
            lax.slice_in_dim(volume, 1, length_a, axis=axis_dim),
            lax.slice_in_dim(volume, length_a - 1, length_a, axis=axis_dim),
        ],
        axis=axis_dim,
    )
    return ahead - volume


def backward_shift(field, axis_dim):
    length_a = field.shape[axis_dim]
    zero_row = jnp.zeros_like(lax.slice_in_dim(field, 0, 1, axis=axis_dim))
    return jnp.concatenate(
        [zero_row, lax.slice_in_dim(field, 0, length_a - 1, axis=axis_dim)], axis=axis_dim
    )


def place_window(partial_value, piece, block_index, start):
    corner = (block_index * SB, start)
    current = lax.dynamic_slice(partial_value, corner, (SB, WIN))
    return lax.dynamic_update_slice(partial_value, current + piece, corner)


def slab_tv(image):
    planes_ext = extended(image, (("vox", 0),), 1)
    slab_planes = image.shape[0]
    is_first = lax.axis_index("vox") == 0
    is_last = lax.axis_index("vox") == lax.axis_size("vox") - 1
    plane_index = jnp.arange(slab_planes + 1)[:, None, None]
    lower = planes_ext[:-1]
    step_z = planes_ext[1:] - planes_ext[:-1]
    step_z = jnp.where(is_last & (plane_index == slab_planes), 0.0, step_z)
    step_y = forward_step(lower, 1)
    step_x = forward_step(lower, 2)
    magnitude = jnp.sqrt(step_z * step_z + step_y * step_y + step_x * step_x + TV_EPS)
    unit_z = jnp.where(is_first & (plane_index == 0), 0.0, step_z / magnitude)
    unit_y = step_y / magnitude
    unit_x = step_x / magnitude
    result = unit_z[:-1] - unit_z[1:]
    result = result + (backward_shift(unit_y, 1) - unit_y)[1:]
    result = result + (backward_shift(unit_x, 2) - unit_x)[1:]
    return result


def on_device(image, weights, block_ids, offsets, counts, measured):
    voxels = image.astype(jnp.bfloat16).reshape(-1)
    blocks = weights[0, 0]
    block_index = block_ids[0, 0]
    starts = offsets[0, 0]
    live_count = counts[0, 0]
    group_sens = SENSORS // lax.axis_size("sen")
    live = (jnp.arange(K_MAX) < live_count).astype(jnp.float32)
    pieces = (
        jnp.einsum("v,kvc->kc", voxels, blocks, preferred_element_type=jnp.float32) * live[:, None]
    )

    def cut_window(source, block_number, start):
        corner = (block_number * SB, start)
        return lax.dynamic_slice(source, corner, (SB, WIN)).reshape(SB * WIN)

    zero_partial = jnp.zeros((group_sens, SAMPLES), jnp.float32)

    def add_masked(slot, partial_value):
        return place_window(
            partial_value, pieces[slot].reshape(SB, WIN), block_index[slot], starts[slot]
        )

    partial_value = lax.fori_loop(0, K_MAX, add_masked, zero_partial)
    whole_measured = lax.all_gather(measured, "vox", axis=1, tiled=True)
    summed = lax.psum(partial_value[None], "vox")
    residual_all = derivative(summed) - whole_measured.astype(jnp.float32)
    adjoint_all = (-derivative(residual_all)).astype(jnp.bfloat16)[0]
    own_rows = measured.shape[1]
    residual = lax.dynamic_slice_in_dim(residual_all, lax.axis_index("vox") * own_rows, own_rows, 1)
    windows = jax.vmap(lambda number, start: cut_window(adjoint_all, number, start))(
        block_index, starts
    )
    windows = windows * live.astype(jnp.bfloat16)[:, None]
    grad_local = jnp.einsum("kc,kvc->v", windows, blocks, preferred_element_type=jnp.float32)
    backprojected = lax.psum(grad_local, "sen").reshape(image.shape)
    image_next = image - STEP_SIZE * (backprojected + TV_WEIGHT * slab_tv(image))
    return (image_next, residual)


def solution(mesh):
    placed = (
        P("vox", None, None),
        P("vox", "sen", None, None, None),
        P("vox", "sen", None),
        P("vox", "sen", None),
        P("vox", "sen"),
        P("sen", "vox", None),
    )
    return jax.shard_map(
        on_device,
        mesh=mesh,
        in_specs=placed,
        out_specs=(P("vox", None, None), P("sen", "vox", None)),
        check_vma=False,
    )
```

profile of v0, /device:TPU:1, one launch (start us, length us, event | category | flops | bytes accessed | tf_op | source)
XLA Modules:
  0.0 1128.4 jit_solution(18124372229311792243)
XLA Ops:
  7.2 4.4 collective-permute-start.1
  11.6 1.4 copy.10
  13.7 0.8 constant_dynamic-update-slice_fusion
  14.5 5.5 fusion.2
  19.9 0.1 bitcast_multiply_fusion
  20.0 0.2 broadcast_in_dim.30
  20.3 0.3 copy-done.2
  20.6 22.0 %while.14 = (s32[]{:T(128)}, f32[256,2048]{1,0:T(8,128)S(1)}, s32[5]{0:T(128)S(1)}, s32[5]{0:T(128)S(1)}, f32[5,1024]{1,0:T(8,128)S(1)}, /*index=5*/s32[]{:T(128)}, s32[1]{0:T(128)}, s32[]{:T(128)}, s32[]{:T(128)}, s32[]{:T(128)}) while((s32[]{:T(128)}, f32[256,2048]{1,0:T(8,128)S(1)}, s32[5]{0:T(128)S(1)}, s32[5]{0:T(128)S(1)}, ...), condition=%wide.region_1.0_spmd, body=%wide.region_0.0_spmd.sunk | while | flops 1033 | bytes 37093 | solution.py:109
  20.6 0.1 squeeze.43
  20.7 0.6 dynamic_slice.41
  21.8 0.6 dynamic_slice.42
  24.0 0.1 dynamic-slice_add_fusion.2
  24.1 0.8 dynamic_update_slice.8
  24.9 0.1 squeeze.43
  25.0 0.6 dynamic_slice.41
  26.1 0.6 dynamic_slice.42
  28.3 0.1 dynamic-slice_add_fusion.2
  28.4 0.9 dynamic_update_slice.8
  29.4 0.1 squeeze.43
  29.4 0.6 dynamic_slice.41
  30.6 0.6 dynamic_slice.42
  32.8 0.1 dynamic-slice_add_fusion.2
  32.8 0.9 dynamic_update_slice.8
  33.9 0.6 dynamic_slice.41
  35.0 0.6 dynamic_slice.42
  37.2 0.1 dynamic-slice_add_fusion.2
  37.3 0.9 dynamic_update_slice.8
  38.3 0.6 dynamic_slice.41
  39.4 0.6 dynamic_slice.42
  41.6 0.1 dynamic-slice_add_fusion.2
  41.7 0.9 dynamic_update_slice.8
  42.7 1.3 copy-done
  44.0 1.3 collective-permute-start
  45.4 0.1 slice.87
  45.5 0.1 slice.86
  45.5 3.6 collective-permute-done
  49.1 0.1 broadcast_select_fusion
  49.2 0.1 fusion.14
  49.3 273.7 %all-gather.2.cloned.1.call-done = bf16[1,256,2048]{2,0,1:T(2,128)(2,1)} async-done(((bf16[1,4,2048]{2,0,1:T(2,128)(2,1)}), bf16[1,256,2048]{2,0,1:T(2,128)(2,1)}) %all-gather.2.cloned.1.call-update) | async-done | bytes 1048592 | tf_op jit(solution)/shard_map/all_gather | solution.py:110
  323.0 717.5 %all-reduce.6.cloned.1.call-done = f32[1,256,2048]{2,1,0:T(8,128)} async-done(((f32[1,256,2048]{2,1,0:T(8,128)}), f32[1,256,2048]{2,1,0:T(8,128)}) %all-reduce.6.cloned.1.call-update) | async-done | bytes 2097168 | tf_op jit(solution)/shard_map/psum | solution.py:111
  1040.5 6.5 convert_subtract_fusion
  1047.0 2.2 fusion.6
  1049.2 10.0 while.15
  1049.3 0.1 constant_dynamic-slice_fusion.3
  1049.3 0.5 fusion.19
  1049.9 1.4 bitcast_dynamic-update-slice_fusion.2
  1051.2 0.1 constant_dynamic-slice_fusion.3
  1051.3 0.5 fusion.19
  1051.9 1.4 bitcast_dynamic-update-slice_fusion.2
  1053.2 0.1 constant_dynamic-slice_fusion.3
  1053.3 0.5 fusion.19
  1053.9 1.4 bitcast_dynamic-update-slice_fusion.2
  1055.2 0.1 constant_dynamic-slice_fusion.3
  1055.3 0.5 fusion.19
  1055.8 1.4 bitcast_dynamic-update-slice_fusion.2
  1057.2 0.1 constant_dynamic-slice_fusion.3
  1057.3 0.5 fusion.19
  1057.8 1.4 bitcast_dynamic-update-slice_fusion.2
  1059.2 0.1 reshape.87
  1059.3 0.1 multiply_bitcast_fusion
  1059.4 6.8 fusion
  1066.2 54.1 %psum.15 = f32[1,2,512]{2,1,0:T(2,128)S(1)} all-reduce(f32[1,2,512]{2,1,0:T(2,128)S(1)} %reshape.88), channel_id=1, replica_groups=mesh['vox'=64,'sen'=4] {'sen'}, use_global_device_ids=true, to_apply=%region_3.4 | all-reduce | flops 1024 | bytes 8192 | tf_op jit(solution)/shard_map/psum | solution.py:121
  1120.3 0.6 constant_dynamic-slice_fusion.1
  1120.9 0.7 multiply_subtract_fusion
  (28 shorter events, 0.4 us)
Async XLA Ops:
  7.2 315.8 %all-gather.2.cloned.1.call-start = ((), (), s32[]{:S(2)}) async-start(), calls=%async_computation.1 | async-start | bytes 2129920 | tf_op jit(solution)/shard_map/all_gather | solution.py:110
  7.2 6.5 collective-permute-start.1
  13.0 1027.5 %all-reduce.6.cloned.1.call-start = ((), (), s32[]{:S(2)}) async-start(), calls=%async_computation | async-start | bytes 4194304 | tf_op jit(solution)/shard_map/psum | solution.py:111
  19.9 0.7 copy-start.2
  19.9 0.7 copy-start.3
  20.0 24.0 %copy-start.1 = (f32[1,2,512]{2,1,0:T(2,128)S(1)}, f32[1,2,512]{2,1,0:T(2,128)}, u32[]{:S(2)}) copy-start(f32[1,2,512]{2,1,0:T(2,128)} %param.8) | copy-start | bytes 12292
  42.7 1.3 copy-start
  44.0 5.1 collective-permute-start
Sparse Core Ops, SparseCore 0:
  13.1 309.8 all-gather.1
  325.6 714.8 all-reduce.5
where the time goes:
time: 1130 us
  waiting for transfers between devices  995 us (88%)
  blocking collectives  54.1 us (5%)
  local copies, waits for them, and re-layouts  24.6 us (2%)
  between operations  14.8 us (1%)
  matrix products  12.3 us (1%)
    psum x1, waiting for transfers between devices, on_device(): summed = lax.psum(partial_value[None], 'vox')  718 us
    all_gather x1, waiting for transfers between devices, on_device(): whole_measured = lax.all_gather(measured, 'vox', axis=1, tiled=True)  274 us
    psum x1, blocking collectives, on_device(): backprojected = lax.psum(grad_local, 'sen').reshape(image.shape)  54.1 us
  transfers between devices with their start and end apart: 4, of which 3 were waited for; matrix products, arithmetic and copies ran while one was open for 2% of the time, Pallas kernels for 0%

commit v1 on v0

--- a/solution.py
+++ b/solution.py
@@ -107,7 +107,9 @@
         )
 
     partial_value = lax.fori_loop(0, K_MAX, add_masked, zero_partial)
-    whole_measured = lax.all_gather(measured, "vox", axis=1, tiled=True)
+    whole_measured = jnp.concatenate(
+        lax.all_to_all(jnp.stack([measured] * lax.axis_size("vox")), "vox", 0, 0), axis=1
+    )
     summed = lax.psum(partial_value[None], "vox")
     residual_all = derivative(summed) - whole_measured.astype(jnp.float32)
     adjoint_all = (-derivative(residual_all)).astype(jnp.bfloat16)[0]

time: 1130 us -> 816 us (0.72)
  waiting for transfers between devices: 995 us -> 666 us
  starting transfers between devices: 5.74 us -> 17.7 us
    all_gather x1 -> x0, waiting for transfers between devices: 274 us -> none  [on_device(): whole_measured = lax.all_gather(measured, 'vox', axis=1, tiled=True)]
    psum x1, waiting for transfers between devices: 718 us -> 635 us  [on_device(): summed = lax.psum(partial_value[None], 'vox')]
    all_to_all x0 -> x1, waiting for transfers between devices: none -> 21.8 us  [on_device(): lax.all_to_all(jnp.stack([measured] * lax.axis_size('vox')), 'vox', 0, 0)]
    all_to_all x0 -> x1, starting transfers between devices: none -> 11.9 us  [on_device(): lax.all_to_all(jnp.stack([measured] * lax.axis_size('vox')), 'vox', 0, 0)]
  transfers between devices with their start and end apart: 4 -> 4, of which waited for: 3 -> 4; matrix products, arithmetic and copies ran while one was open for 2% -> 0% of each run, Pallas kernels for 0% -> 0%
where the time goes in v1:
time: 816 us; the launch traced here: 815 us
  waiting for transfers between devices  666 us (82%)
  blocking collectives  54.1 us (7%)
  local copies, waits for them, and re-layouts  26.6 us (3%)
  starting transfers between devices  17.7 us (2%)
  between operations  14.8 us (2%)
  loops' own time  12.9 us (2%)
  matrix products  12.3 us (2%)
  other arithmetic  10.7 us (1%)
    psum x1, waiting for transfers between devices, on_device(): summed = lax.psum(partial_value[None], 'vox')  635 us
    psum x1, blocking collectives, on_device(): backprojected = lax.psum(grad_local, 'sen').reshape(image.shape)  54.1 us
    all_to_all x1, waiting for transfers between devices, on_device(): lax.all_to_all(jnp.stack([measured] * lax.axis_size('vox')), 'vox', 0, 0)  21.8 us
  transfers between devices with their start and end apart: 4, of which 4 were waited for; matrix products, arithmetic and copies ran while one was open for 0% of the time, Pallas kernels for 0%

profile of v1, /device:TPU:1, one launch (start us, length us, event | category | flops | bytes accessed | tf_op | source)
XLA Modules:
  0.0 815.2 jit_solution(1939579133420188202)
XLA Ops:
  7.2 4.4 collective-permute-start.1
  12.2 0.3 collective-permute-done.1
  12.5 0.8 constant_dynamic-update-slice_fusion
  13.3 5.5 fusion.2
  18.8 0.1 bitcast_multiply_fusion
  18.9 0.2 broadcast_in_dim.30
  19.1 0.3 copy-done.3
  19.5 24.3 %while.14 = (s32[]{:T(128)}, f32[256,2048]{1,0:T(8,128)S(1)}, s32[5]{0:T(128)S(1)}, s32[5]{0:T(128)S(1)}, f32[5,1024]{1,0:T(8,128)S(1)}, /*index=5*/s32[]{:T(128)}, s32[1]{0:T(128)}, s32[]{:T(128)}, s32[]{:T(128)}, s32[]{:T(128)}) while((s32[]{:T(128)}, f32[256,2048]{1,0:T(8,128)S(1)}, s32[5]{0:T(128)S(1)}, s32[5]{0:T(128)S(1)}, ...), condition=%wide.region_1.0_spmd, body=%wide.region_0.0_spmd.sunk | while | flops 1033 | bytes 37085 | solution.py:109
  19.5 0.6 dynamic_slice.41
  20.7 0.6 dynamic_slice.42
  23.3 0.1 dynamic-slice_add_fusion.2
  23.4 0.8 dynamic_update_slice.8
  24.2 0.6 dynamic_slice.41
  25.4 0.6 dynamic_slice.42
  28.1 0.1 dynamic-slice_add_fusion.2
  28.2 0.9 dynamic_update_slice.8
  29.1 0.6 dynamic_slice.41
  30.3 0.6 dynamic_slice.42
  33.0 0.1 dynamic-slice_add_fusion.2
  33.0 0.9 dynamic_update_slice.8
  34.0 0.6 dynamic_slice.41
  35.2 0.6 dynamic_slice.42
  37.9 0.1 dynamic-slice_add_fusion.2
  37.9 0.9 dynamic_update_slice.8
  38.9 0.6 dynamic_slice.41
  40.1 0.6 dynamic_slice.42
  42.8 0.1 dynamic-slice_add_fusion.2
  42.8 0.9 dynamic_update_slice.8
  43.8 1.3 copy-done
  45.1 1.5 stack.2
  46.6 11.9 %all-to-all-start = ((bf16[64,1,4,2048]{3,2,1,0:T(4,128)(2,1)}), bf16[64,1,4,2048]{3,2,1,0:T(4,128)(2,1)S(1)}, u32[]{:S(2)}, u32[]{:S(2)}) async-start(bf16[64,1,4,2048]{3,2,1,0:T(4,128)(2,1)} %stack.2), calls=%async_computation | async-start | bytes 2097152 | tf_op jit(solution)/shard_map/all_to_all | solution.py:111
  58.6 1.3 collective-permute-start
  59.9 0.1 slice.86
  60.0 0.1 slice.87
  60.1 8.7 %collective-permute-done = f32[1,2,512]{2,1,0:T(2,128)S(1)} collective-permute-done((f32[1,2,512]{2,1,0:T(2,128)S(1)}, f32[1,2,512]{2,1,0:T(2,128)S(1)}, u32[]{:S(2)}, u32[]{:S(2)}) %collective-permute-start) | collective-permute-done | bytes 4128 | tf_op jit(solution)/shard_map/ppermute | solution.py:25
  68.8 0.1 broadcast_select_fusion
  68.9 0.1 fusion.14
  69.0 21.8 %all-to-all-done = bf16[64,1,4,2048]{3,2,1,0:T(4,128)(2,1)S(1)} async-done(((bf16[64,1,4,2048]{3,2,1,0:T(4,128)(2,1)}), bf16[64,1,4,2048]{3,2,1,0:T(4,128)(2,1)S(1)}, u32[]{:S(2)}, u32[]{:S(2)}) %all-to-all-start) | async-done | bytes 1048608 | tf_op jit(solution)/shard_map/all_to_all | solution.py:111
  90.8 1.4 reshape.126
  92.2 635.3 %all-reduce.6.cloned.1.call-done = f32[1,256,2048]{2,1,0:T(8,128)} async-done(((f32[1,256,2048]{2,1,0:T(8,128)}), f32[1,256,2048]{2,1,0:T(8,128)}) %all-reduce.6.cloned.1.call-update) | async-done | bytes 2097168 | tf_op jit(solution)/shard_map/psum | solution.py:113
  727.5 6.3 add_subtract_fusion
  733.7 2.2 fusion.6
  736.0 10.0 %while.15 = (s32[]{:T(128)}, bf16[256,2048]{1,0:T(8,128)(2,1)S(1)}, s32[5,2]{0,1:T(2,128)S(1)}, bf16[5,16,64]{2,1,0:T(8,128)(2,1)S(1)}, s32[]{:T(128)}) while((s32[]{:T(128)}, bf16[256,2048]{1,0:T(8,128)(2,1)S(1)}, s32[5,2]{0,1:T(2,128)S(1)}, bf16[5,16,64]{2,1,0:T(8,128)(2,1)S(1)}, s32[]{:T(128)}) %tuple.55), condition=%wide.while_cond, body=%wide.while_body.sunk | while | flops 2 | bytes 8301 | solution.py:100
  736.0 0.1 constant_dynamic-slice_fusion.3
  736.1 0.5 fusion.19
  736.6 1.4 bitcast_dynamic-update-slice_fusion.2
  738.0 0.1 constant_dynamic-slice_fusion.3
  738.1 0.5 fusion.19
  738.6 1.4 bitcast_dynamic-update-slice_fusion.2
  740.0 0.1 constant_dynamic-slice_fusion.3
  740.0 0.5 fusion.19
  740.6 1.4 bitcast_dynamic-update-slice_fusion.2
  742.0 0.1 constant_dynamic-slice_fusion.3
  742.0 0.5 fusion.19
  742.6 1.4 bitcast_dynamic-update-slice_fusion.2
  744.0 0.1 constant_dynamic-slice_fusion.3
  744.0 0.5 fusion.19
  744.6 1.4 bitcast_dynamic-update-slice_fusion.2
  746.0 0.1 reshape.105
  746.1 0.1 multiply_bitcast_fusion
  746.1 6.8 fusion
  752.9 54.1 %psum.15 = f32[1,2,512]{2,1,0:T(2,128)S(1)} all-reduce(f32[1,2,512]{2,1,0:T(2,128)S(1)} %reshape.106), channel_id=1, replica_groups=mesh['vox'=64,'sen'=4] {'sen'}, use_global_device_ids=true, to_apply=%region_3.4 | all-reduce | flops 1024 | bytes 8192 | tf_op jit(solution)/shard_map/psum | solution.py:123
  807.0 0.6 constant_dynamic-slice_fusion.1
  807.6 0.7 multiply_subtract_fusion
  (30 shorter events, 0.6 us)
Async XLA Ops:
  7.2 720.3 %all-reduce.6.cloned.1.call-start = ((), (), s32[]{:S(2)}) async-start(), calls=%async_computation.1 | async-start | bytes 4194304 | tf_op jit(solution)/shard_map/psum | solution.py:113
  7.2 5.3 collective-permute-start.1
  18.8 0.7 copy-start.3
  18.8 0.7 copy-start.4
  18.9 26.3 %copy-start.2 = (bf16[1,4,2048]{2,1,0:T(4,128)(2,1)S(1)}, bf16[1,4,2048]{2,1,0:T(4,128)(2,1)}, u32[]{:S(2)}) copy-start(bf16[1,4,2048]{2,1,0:T(4,128)(2,1)} %param.13) | copy-start | bytes 49156
  43.8 1.3 copy-start
  45.1 13.5 %copy-start.1 = (f32[1,2,512]{2,1,0:T(2,128)S(1)}, f32[1,2,512]{2,1,0:T(2,128)}, u32[]{:S(2)}) copy-start(f32[1,2,512]{2,1,0:T(2,128)} %param.8) | copy-start | bytes 12292
  46.6 44.1 %all-to-all-start = ((bf16[64,1,4,2048]{3,2,1,0:T(4,128)(2,1)}), bf16[64,1,4,2048]{3,2,1,0:T(4,128)(2,1)S(1)}, u32[]{:S(2)}, u32[]{:S(2)}) async-start(bf16[64,1,4,2048]{3,2,1,0:T(4,128)(2,1)} %stack.2), calls=%async_computation | async-start | bytes 2097152 | tf_op jit(solution)/shard_map/all_to_all | solution.py:111
  58.6 10.2 %collective-permute-start = (f32[1,2,512]{2,1,0:T(2,128)S(1)}, f32[1,2,512]{2,1,0:T(2,128)S(1)}, u32[]{:S(2)}, u32[]{:S(2)}) collective-permute-start(f32[1,2,512]{2,1,0:T(2,128)S(1)} %copy-done.1), channel_id=1, source_target_pairs={{4,0},{8,4},{12,8},{16,12},{20,16},{24,20},{28,24},{32,28},{36,32}... | collective-permute-start | bytes 12296 | tf_op jit(solution)/shard_map/ppermute | solution.py:25
Sparse Core Ops, SparseCore 0:
  45.2 682.1 all-reduce.5
